TPU v7x, 32 devices: a whole 2x2x4 slice. The times are simulated.
32 devices in a mesh: row: 4 (over x, core), col: 8 (over z, y).
Axes of the slice: x: 2, y: 2, z: 4, core: 2. Of those that a mesh axis runs over, the one named last changes fastest.
Arguments:
- coords: float32 [4, 4096], P(None, ('row', 'col')), may hold values from 0 to 1, as said below
- values: float32 [512, 4096], P(None, ('row', 'col')), may hold values from -6 to 6
- coarse_coords: float32 [4, 512], P(None, ('row', 'col')), may hold values from 0 to 1, as said below
- coarse_values: float32 [512, 512], P(None, ('row', 'col')), may hold values from -6 to 6
- fine_index: int32 [32, 128], P(('row', 'col')), may hold values from 0 to 127, as said below
- coarse_index: int32 [32, 384], P(('row', 'col')), may hold values from 0 to 511, as said below
- log_params: float32 [6], replicated, may hold values from -0.5 to 0.5
Outputs:
- step: float32 [6], replicated
- whitened: float32 [512, 4096], P(None, ('row', 'col'))
Inputs may be any that keep to these rules, and one draw needn't show every extreme that they name: `fine_index`: in each row the first 64 entries are distinct, and so are the last 64. `coarse_index`: the entries of each row are distinct; in each row at most 16 entries lie in one tile (j // 16), and some tile holds exactly 16 of them. `coarse_coords`: coarse point j lies in tile j // 16; for tile (r, c) its longitude lies in [c / 8, (c + 1) / 8) and its latitude in [r / 4, (r + 1) / 4), elevation and time in [0, 1). `coords`: fine point p lies in tile p // 128, placed as for the coarse points.
All inputs are finite; a program needn't handle non-finite values.
Results may differ from a plain program's by a relative error of at most 0.0003.
Values sent between devices are 32-bit elements; how exact they have to be, the bound alone decides.
A program may use at most 192 MiB of HBM per device.

v0:
```python
import math

import jax
import jax.numpy as jnp
from jax import lax
from jax.sharding import PartitionSpec as P

HIGH = lax.Precision.HIGHEST
ROOT_FIVE = math.sqrt(5.0)
NUGGET = 0.2
RANGE_BASE = (0.5, 0.5, 0.5, 0.5)


def shifted(value, axis, steps):
    count = lax.axis_size(axis)
    first, last = (max(0, -steps), min(count, count - steps))
    return lax.ppermute(value, axis, [(source, source + steps) for source in range(first, last)])


def passed_along(block, axis, distance):
    devices = range(lax.axis_size(axis))
    route = [((i - distance) % len(devices), i) for i in devices]
    return lax.ppermute(block, axis, route)


def local_covariance(joint_coords, live, theta):
    count = joint_coords.shape[1]
    scale = jnp.exp(theta[1:5]) * jnp.array(RANGE_BASE)
    scaled = joint_coords / scale[:, None]
    diff = scaled[:, :, None] - scaled[:, None, :]
    squares = diff * diff
    dist = jnp.sqrt(jnp.sum(squares, axis=0))
    root = ROOT_FIVE * dist
    decay = jnp.exp(-root)
    variance = jnp.exp(theta[0])
    kernel = variance * (1.0 + root + root * root / 3.0) * decay
    common = variance * (5.0 / 3.0) * (1.0 + root) * decay
    paired = live[:, None] * live[None, :]
    ident = jnp.eye(count, dtype=jnp.float32)
    nugget = NUGGET * jnp.exp(theta[5])
    cov = paired * kernel + (live * nugget + 1.0 - live)[:, None] * ident
    derivs = jnp.concatenate(
        [
            (paired * kernel)[None],
            (paired * common)[None] * squares,
            ((live * nugget)[:, None] * ident)[None],
        ],
        axis=0,
    )
    return (cov, derivs)


def fisher_terms(cov, derivs, lead, reps):
    count = cov.shape[0]
    ident = jnp.eye(count, dtype=jnp.float32)
    factor = jnp.linalg.cholesky(cov)
    inverse = jax.scipy.linalg.solve_triangular(factor, ident, lower=True)
    joint_prec = jnp.dot(inverse.T, inverse, precision=HIGH)
    lead_inv = inverse[:lead, :lead]
    lead_prec = jnp.dot(lead_inv.T, lead_inv, precision=HIGH)
    joint_prod = jnp.einsum("ab,ibc->iac", joint_prec, derivs, precision=HIGH)
    lead_prod = jnp.einsum("ab,ibc->iac", lead_prec, derivs[:, :lead, :lead], precision=HIGH)
    joint_fish = jnp.einsum("iab,jba->ij", joint_prod, joint_prod, precision=HIGH)
    lead_fish = jnp.einsum("iab,jba->ij", lead_prod, lead_prod, precision=HIGH)
    fisher = reps * 0.5 * (joint_fish - lead_fish)
    traces = jnp.trace(joint_prod, axis1=1, axis2=2) - jnp.trace(lead_prod, axis1=1, axis2=2)
    return (inverse, fisher, traces)


def score_terms(inverse, derivs, joint_values, traces, lead, reps):
    white = jnp.dot(joint_values, inverse.T, precision=HIGH)
    alpha = jnp.dot(white, inverse, precision=HIGH)
    lead_alpha = jnp.dot(white[:, :lead], inverse[:lead, :lead], precision=HIGH)
    joint_quad = jnp.sum(
        jnp.einsum("rn,inm->irm", alpha, derivs, precision=HIGH) * alpha[None], axis=(1, 2)
    )
    lead_quad = jnp.sum(
        jnp.einsum("rn,inm->irm", lead_alpha, derivs[:, :lead, :lead], precision=HIGH)
        * lead_alpha[None],
        axis=(1, 2),
    )
    grad = 0.5 * (joint_quad - lead_quad) - 0.5 * reps * traces
    return (grad, white[:, lead:])


def body(coords, values, coarse_coords, coarse_values, fine_index, coarse_index, log_params):
    half = fine_index.shape[1] // 2
    reps = values.shape[0]
    block_size = coords.shape[1]
    pick_upper = fine_index[0, :half]
    pick_left = fine_index[0, half:]
    wanted = coarse_index[0]
    num_coarse = wanted.shape[0]
    lead = num_coarse + 2 * half
    upper_coords, upper_values = shifted((coords, values), "row", 1)
    left_coords, left_values = passed_along((coords, values), "col", 1)
    upper_coords = jnp.take(upper_coords, pick_upper, axis=1)
    upper_values = jnp.take(upper_values, pick_upper, axis=1)
    left_coords = jnp.take(left_coords, pick_left, axis=1)
    left_values = jnp.take(left_values, pick_left, axis=1)
    piece_coords = lax.all_gather(coarse_coords, ("row", "col"), axis=1, tiled=True)
    piece_values = lax.all_gather(coarse_values, ("row", "col"), axis=1, tiled=True)
    width = piece_coords.shape[1]
    onehot = (wanted[None, :] == jnp.arange(width, dtype=jnp.int32)[:, None]).astype(jnp.float32)
    picked_coords = jnp.dot(piece_coords, onehot, precision=HIGH)
    picked_values = jnp.dot(piece_values, onehot, precision=HIGH)
    upper_live = (lax.axis_index("row") > 0).astype(jnp.float32)
    joint_coords = jnp.concatenate([picked_coords, upper_coords, left_coords, coords], axis=1)
    joint_values = jnp.concatenate([picked_values, upper_values, left_values, values], axis=1)
    live = jnp.concatenate(
        [
            jnp.ones((num_coarse,), jnp.float32),
            upper_live * jnp.ones((half,), jnp.float32),
            jnp.ones((half + block_size,), jnp.float32),
        ]
    )
    cov, derivs = local_covariance(joint_coords, live, log_params)
    inverse, fisher, traces = fisher_terms(cov, derivs, lead, reps)
    grad, white = score_terms(inverse, derivs, joint_values, traces, lead, reps)
    grad, fisher = lax.psum((grad, fisher), ("row", "col"))
    step = jax.scipy.linalg.cho_solve((jnp.linalg.cholesky(fisher), True), grad)
    return (step, white)


def solution(mesh):
    in_specs = (
        P(None, ("row", "col")),
        P(None, ("row", "col")),
        P(None, ("row", "col")),
        P(None, ("row", "col")),
        P(("row", "col"), None),
        P(("row", "col"), None),
        P(),
    )
    out_specs = (P(), P(None, ("row", "col")))
    return jax.shard_map(body, mesh=mesh, in_specs=in_specs, out_specs=out_specs, check_vma=False)
```

profile of v0, /device:TPU:0, one launch (start us, length us, event | category | flops | bytes accessed | tf_op | source)
XLA Modules:
  0.0 581.0 jit_solution(4296260236476704063)
XLA Ops:
  8.0 3.0 collective-permute-start.1
  15.8 3.7 collective-permute-start.2
  24.7 65.1 %all-gather = f32[32,16,4]{1,2,0:T(4,128)S(1)} all-gather(f32[1,16,4]{1,2,0:T(4,128)S(1)} %bitcast.157), channel_id=1, replica_groups=mesh['row'=4,'col'=8] {'row','col'}, dimensions={0}, use_global_device_ids=true | all-gather | bytes 8448 | tf_op jit(solution)/shard_map/all_gather | solution.py:101
  97.0 3.2 negate_exponential_fusion
  109.0 3.2 copy.65
  115.6 11.7 %cholesky.146 = f32[128,128]{1,0:T(8,128)S(1)} custom-call(f32[128,128]{1,0:T(8,128)S(1)} %cholesky.372), custom_call_target="Cholesky" | custom-call | tf_op jit(solution)/shard_map/jit(cholesky)/cholesky | solution.py:56
  129.6 11.3 %custom-call.49 = f32[1,128,128]{1,2,0:T(8,128)} custom-call(f32[1,128,128]{2,1,0:T(8,128)} %get-tuple-element.43), custom_call_target="InvertDiagBlocksLowerTriangular" | custom-call | tf_op jit(solution)/shard_map/jit(cholesky)/cholesky | solution.py:56
  143.8 13.2 %cholesky.171 = f32[128,128]{1,0:T(8,128)} custom-call(f32[128,128]{1,0:T(8,128)} %cholesky.376), custom_call_target="Cholesky" | custom-call | tf_op jit(solution)/shard_map/jit(cholesky)/cholesky | solution.py:56
  159.0 11.4 %custom-call.50 = f32[1,128,128]{1,2,0:T(8,128)} custom-call(f32[1,128,128]{2,1,0:T(8,128)} %get-tuple-element.40), custom_call_target="InvertDiagBlocksLowerTriangular" | custom-call | tf_op jit(solution)/shard_map/jit(cholesky)/cholesky | solution.py:56
  173.4 13.2 %cholesky.317 = f32[128,128]{1,0:T(8,128)} custom-call(f32[128,128]{1,0:T(8,128)} %cholesky.381), custom_call_target="Cholesky" | custom-call | tf_op jit(solution)/shard_map/jit(cholesky)/cholesky | solution.py:56
  188.6 11.3 %custom-call.51 = f32[1,128,128]{1,2,0:T(8,128)} custom-call(f32[1,128,128]{2,1,0:T(8,128)} %get-tuple-element.37), custom_call_target="InvertDiagBlocksLowerTriangular" | custom-call | tf_op jit(solution)/shard_map/jit(cholesky)/cholesky | solution.py:56
  202.8 13.4 %cholesky.336 = f32[128,128]{1,0:T(8,128)} custom-call(f32[128,128]{1,0:T(8,128)} %cholesky.386), custom_call_target="Cholesky" | custom-call | tf_op jit(solution)/shard_map/jit(cholesky)/cholesky | solution.py:56
  218.2 11.3 %custom-call.52 = f32[1,128,128]{1,2,0:T(8,128)} custom-call(f32[1,128,128]{2,1,0:T(8,128)} %get-tuple-element.34), custom_call_target="InvertDiagBlocksLowerTriangular" | custom-call | tf_op jit(solution)/shard_map/jit(cholesky)/cholesky | solution.py:56
  231.5 12.5 %cholesky.353 = f32[128,128]{1,0:T(8,128)S(1)} custom-call(f32[128,128]{1,0:T(8,128)} %convolution_subtract_fusion.6), custom_call_target="Cholesky" | custom-call | tf_op jit(solution)/shard_map/jit(cholesky)/cholesky | solution.py:56
  253.1 13.1 %while.1 = (s32[]{:T(128)}, f32[640,640]{1,0:T(8,128)S(1)}, s32[5,2]{0,1:T(2,128)S(1)}, f32[5,128,128]{2,1,0:T(8,128)}, s32[]{:T(128)}) while((s32[]{:T(128)}, f32[640,640]{1,0:T(8,128)S(1)}, s32[5,2]{0,1:T(2,128)S(1)}, f32[5,128,128]{2,1,0:T(8,128)}, s32[]{:T(128)}) %tuple.51), condition=%wide.while_cond, body=%wide.while_body.sunk | while | flops 2 | bytes 132205 | solution.py:57
  267.4 50.9 %custom-call.53 = f32[5,128,128]{1,2,0:T(8,128)} custom-call(f32[5,128,128]{2,1,0:T(8,128)} %get-tuple-element.11), custom_call_target="InvertDiagBlocksLowerTriangular" | custom-call | tf_op jit(solution)/shard_map/jit(_solve_triangular)/triangular_solve | solution.py:57
  328.8 2.9 convolution_bitcast_fusion.1
  332.2 6.2 %fusion.100 = f32[640,640]{1,0:T(8,128)} fusion(f32[640,640]{1,0:T(8,128)S(1)} %convolution_dynamic-update-slice_fusion), kind=kOutput, calls=%fused_computation.189 | convolution fusion | flops 3145728000 | bytes 3276800 | tf_op jit(solution)/shard_map/dot_general | solution.py:58
  338.5 3.8 fusion.7
  345.2 30.9 %select_reduce_fusion = (f32[6]{0:T(128)S(1)}, f32[6,640,640]{1,2,0:T(8,128)}) fusion(pred[640,640]{0,1:T(8,128)(4,1)S(1)} %copy-done.22, f32[640,640]{1,0:T(8,128)} %fusion.100, f32[1,640,640]{1,2,0:T(8,128)S(1)} %copy-done.4, f32[4,640,640]{1,2,0:T(8,128)} %fusion.7, f32[1,640,640]{1,2,0:T(8,128)} %copy.64), kind=kOutput, calls=%fused_computation.9 | convolution fusion | flops 18884198400 | bytes 21708824 | tf_op jit(solution)/shard_map/ab,ibc->iac/dot_general | solution.py:61
  376.0 14.5 %copy.67 = f32[6,640,640]{2,0,1:T(8,128)} copy(f32[6,640,640]{1,2,0:T(8,128)} %get-tuple-element.63) | data formatting | bytes 19660800 | tf_op jit(solution)/shard_map/ab,ibc->iac/transpose | solution.py:61
  390.5 16.0 %select_reduce_fusion.1 = (f32[6]{0:T(128)S(1)}, f32[6,512,512]{1,2,0:T(8,128)}) fusion(pred[512,512]{0,1:T(8,128)(4,1)S(1)} %copy-done.17, f32[512,512,1]{1,0,2:T(8,128)S(1)} %copy-done.18, f32[1,640,640]{1,2,0:T(8,128)S(1)} %copy-done.4, f32[4,640,640]{1,2,0:T(8,128)} %fusion.7, f32[1,640,640]{1,2,0:T(8,128)} %copy.64), kind=kOutput, calls=%fused_computation.22 | convolution fusion | flops 9669967872 | bytes 17432600 | tf_op jit(solution)/shard_map/ab,ibc->iac/dot_general | solution.py:62
  406.5 9.8 %copy.69 = f32[6,512,512]{2,0,1:T(8,128)} copy(f32[6,512,512]{1,2,0:T(8,128)} %get-tuple-element.65) | data formatting | bytes 12582912 | tf_op jit(solution)/shard_map/ab,ibc->iac/transpose | solution.py:62
  416.3 34.7 %fusion.36 = f32[6,6]{0,1:T(8,128)S(1)} fusion(f32[6,640,640]{2,0,1:T(8,128)} %copy.67, f32[6,640,640]{1,2,0:T(8,128)} %get-tuple-element.63), kind=kOutput, calls=%fused_computation.72 | convolution fusion | flops 176947200 | bytes 19660944 | tf_op jit(solution)/shard_map/iab,jba->ij/dot_general | solution.py:63
  451.1 18.9 %fusion.42 = f32[6,6]{0,1:T(8,128)S(1)} fusion(f32[6,6]{0,1:T(8,128)S(1)} %fusion.36, f32[6,512,512]{2,0,1:T(8,128)S(1)} %copy-done, f32[6,512,512]{1,2,0:T(8,128)S(1)} %bitcast.156), kind=kOutput, calls=%fused_computation.74 | convolution fusion | flops 113246280 | bytes 12583200 | tf_op jit(solution)/shard_map/iab,jba->ij/dot_general | solution.py:64
  475.2 7.4 %fusion.21 = f32[512,640]{1,0:T(8,128)S(1)} fusion(f32[640,640]{1,0:T(8,128)S(1)} %copy-done.2, f32[512,128]{0,1:T(8,128)} %copy.75, f32[512,64]{0,1:T(8,128)S(1)} %select_bitcast_fusion, f32[512,64]{0,1:T(8,128)S(1)} %select_bitcast_fusion.1, f32[512,384]{0,1:T(8,128)S(1)} %convolution_bitcast_fusion.2), kind=kOutput, calls=%fused_computation.48 | convolution fusion | flops 2517565440 | bytes 4259840 | tf_op jit(solution)/shard_map/dot_general | solution.py:71
  482.6 4.8 fusion.101
  487.4 3.0 fusion.45
  490.4 2.9 copy.78
  493.4 21.7 %fusion.4 = f32[6]{0:T(128)S(1)} fusion(f32[512,640]{0,1:T(8,128)} %copy.78, f32[1,640,640]{1,2,0:T(8,128)S(1)} %copy-done.5, f32[4,640,640]{1,2,0:T(8,128)} %fusion.7, f32[1,640,640]{1,2,0:T(8,128)} %copy.64, f32[512,640]{1,0:T(8,128)} %fusion.101), kind=kOutput, calls=%fused_computation.13 | convolution fusion | flops 15108341760 | bytes 12451864 | tf_op jit(solution)/shard_map/rn,inm->irm/dot_general | solution.py:75
  517.6 14.1 %fusion.9 = f32[6]{0:T(128)S(1)} fusion(f32[512,512]{0,1:T(8,128)} %copy.79, f32[1,640,640]{1,2,0:T(8,128)S(1)} %copy-done.5, f32[4,640,640]{1,2,0:T(8,128)} %fusion.7, f32[1,640,640]{1,2,0:T(8,128)} %copy.64, f32[512,512]{1,0:T(8,128)} %fusion.45), kind=kOutput, calls=%fused_computation.21 | convolution fusion | flops 9669967872 | bytes 11927576 | tf_op jit(solution)/shard_map/rn,inm->irm/dot_general | solution.py:78
  532.4 38.0 %all-reduce.1 = (f32[6,6]{0,1:T(8,128)S(1)}, f32[6]{0:T(128)S(1)}) all-reduce(f32[6,6]{0,1:T(8,128)S(1)} %fusion.42, f32[6]{0:T(128)S(1)} %multiply_subtract_fusion), channel_id=1, replica_groups=mesh['row'=4,'col'=8] {'row','col'}, use_global_device_ids=true, to_apply=%region_11.13 | all-reduce | flops 42 | bytes 336 | tf_op jit(solution)/shard_map/psum | solution.py:120
  (194 shorter events, 93.3 us)
Async XLA Ops:
  7.2 17.4 %copy-start.36 = (s32[1,128]{1,0:T(1,128)S(1)}, s32[1,128]{1,0:T(1,128)}, u32[]{:S(2)}) copy-start(s32[1,128]{1,0:T(1,128)} %param.16) | copy-start | bytes 1540
  7.2 17.5 %copy-start.35 = (f32[4,16]{1,0:T(4,128)S(1)}, f32[4,16]{1,0:T(4,128)}, u32[]{:S(2)}) copy-start(f32[4,16]{1,0:T(4,128)} %param.14) | copy-start | bytes 772
  7.2 82.7 %copy-start.37 = (s32[1,384]{1,0:T(1,128)S(1)}, s32[1,384]{1,0:T(1,128)}, u32[]{:S(2)}) copy-start(s32[1,384]{1,0:T(1,128)} %param.17) | copy-start | bytes 4612
  7.2 465.7 %all-gather.3.cloned.1.call-start = ((), (), s32[]{:S(2)}) async-start(), calls=%async_computation | async-start | bytes 1081344 | tf_op jit(solution)/shard_map/all_gather | solution.py:102
  8.0 86.8 %collective-permute-start.1 = (f32[4,128]{0,1:T(8,128)S(1)}, f32[4,128]{0,1:T(8,128)S(1)}, u32[]{:S(2)}, u32[]{:S(2)}) collective-permute-start(f32[4,128]{0,1:T(8,128)S(1)} %copy.58), channel_id=1, source_target_pairs={{7,0},{0,1},{1,2},{2,3},{3,4},{4,5},{5,6},{6,7},{15,8},{8,9},{9,10... | collective-permute-start | bytes 6152 | tf_op jit(solution)/shard_map/ppermute | solution.py:23
  11.1 84.4 %collective-permute-start = (f32[4,128]{0,1:T(8,128)S(1)}, f32[4,128]{0,1:T(8,128)S(1)}, u32[]{:S(2)}, u32[]{:S(2)}) collective-permute-start(f32[4,128]{0,1:T(8,128)S(1)} %copy.58), channel_id=1, source_target_pairs={{0,8},{8,16},{16,24},{1,9},{9,17},{17,25},{2,10},{10,18},{18,26},{... | collective-permute-start | bytes 6152 | tf_op jit(solution)/shard_map/ppermute | solution.py:17
  14.3 455.7 %collective-permute-start.3 = (f32[512,128]{0,1:T(8,128)}, f32[512,128]{0,1:T(8,128)}, u32[]{:S(2)}, u32[]{:S(2)}) collective-permute-start(f32[512,128]{0,1:T(8,128)} %copy.75), channel_id=1, source_target_pairs={{7,0},{0,1},{1,2},{2,3},{3,4},{4,5},{5,6},{6,7},{15,8},{8,9},{9,10... | collective-permute-start | bytes 786440 | tf_op jit(solution)/shard_map/ppermute | solution.py:23
  15.8 456.0 %collective-permute-start.2 = (f32[512,128]{0,1:T(8,128)}, f32[512,128]{0,1:T(8,128)S(1)}, u32[]{:S(2)}, u32[]{:S(2)}) collective-permute-start(f32[512,128]{0,1:T(8,128)} %copy.75), channel_id=1, source_target_pairs={{0,8},{8,16},{16,24},{1,9},{9,17},{17,25},{2,10},{10,18},{18,26},{... | collective-permute-start | bytes 786440 | tf_op jit(solution)/shard_map/ppermute | solution.py:17
  19.7 73.2 %copy-start.14 = (pred[640,640]{1,0:T(32,128)(4,1)}, pred[640,640]{1,0:T(32,128)(4,1)S(1)}, u32[]{:S(2)}) copy-start(pred[640,640]{1,0:T(32,128)(4,1)S(1)} %iota_compare_fusion.1) | copy-start | bytes 1228804
  23.1 73.1 %copy-start.26 = (f32[4,128]{1,0:T(4,128)S(1)}, f32[4,128]{1,0:T(4,128)}, u32[]{:S(2)}) copy-start(f32[4,128]{1,0:T(4,128)} %param.12) | copy-start | bytes 6148
  24.6 72.4 %copy-start.31 = (pred[64]{0:T(512)(128)(4,1)}, pred[64]{0:T(512)(128)(4,1)S(1)}, u32[]{:S(2)}) copy-start(pred[64]{0:T(512)(128)(4,1)S(1)} %get-tuple-element.22) | copy-start | bytes 196
  24.6 72.4 %copy-start.33 = (pred[64]{0:T(512)(128)(4,1)}, pred[64]{0:T(512)(128)(4,1)S(1)}, u32[]{:S(2)}) copy-start(pred[64]{0:T(512)(128)(4,1)S(1)} %get-tuple-element.50) | copy-start | bytes 196
  24.6 71.6 %copy-start.30 = (s32[1024]{0:T(1024)}, s32[1024]{0:T(1024)S(1)}, u32[]{:S(2)}) copy-start(s32[1024]{0:T(1024)S(1)} %pad_clamp_fusion) | copy-start | bytes 12292
  24.6 71.5 %copy-start.29 = (s32[1024]{0:T(1024)}, s32[1024]{0:T(1024)S(1)}, u32[]{:S(2)}) copy-start(s32[1024]{0:T(1024)S(1)} %pad_clamp_fusion.1) | copy-start | bytes 12292
  89.9 7.1 %copy-start.27 = (s32[384]{0:T(512)}, s32[384]{0:T(512)S(1)}, u32[]{:S(2)}) copy-start(s32[384]{0:T(512)S(1)} %reduce.36) | copy-start | bytes 4612
  109.0 3.2 copy-start.25
  115.6 25.2 %copy-start.10 = (f32[640,640]{1,0:T(8,128)S(1)}, f32[640,640]{1,0:T(8,128)}, u32[]{:S(2)}) copy-start(f32[640,640]{1,0:T(8,128)} %copy-done.9) | copy-start | bytes 4915204
  266.2 56.1 %copy-start.8 = (f32[640,640]{1,0:T(8,128)S(1)}, f32[640,640]{1,0:T(8,128)}, u32[]{:S(2)}) copy-start(f32[640,640]{1,0:T(8,128)} %fusion.53) | copy-start | bytes 4915204
  319.5 4.4 copy-start.23
  322.3 6.5 %copy-start.6 = (f32[128,640]{1,0:T(8,128)}, f32[128,640]{1,0:T(8,128)S(1)}, u32[]{:S(2)}) copy-start(f32[128,640]{1,0:T(8,128)S(1)} %get-tuple-element.57) | copy-start | bytes 983044
  324.4 4.4 copy-start.12
  326.8 5.0 copy-start.15
  332.2 6.2 %copy-start.1 = (f32[640,640]{1,0:T(8,128)}, f32[640,640]{1,0:T(8,128)S(1)}, u32[]{:S(2)}) copy-start(f32[640,640]{1,0:T(8,128)S(1)} %convolution_dynamic-update-slice_fusion) | copy-start | bytes 4915204
  332.2 6.2 %copy-start.3 = (f32[640,640]{0,1:T(8,128)S(1)}, f32[640,640]{0,1:T(8,128)}, u32[]{:S(2)}) copy-start(f32[640,640]{0,1:T(8,128)} %get-tuple-element.30) | copy-start | bytes 4915204
  376.0 14.5 %copy-start.17 = (pred[512,512]{0,1:T(8,128)(4,1)S(1)}, pred[512,512]{0,1:T(8,128)(4,1)}, u32[]{:S(2)}) copy-start(pred[512,512]{0,1:T(8,128)(4,1)} %iota_compare_fusion.4) | copy-start | bytes 786436
  376.0 14.5 %copy-start.18 = (f32[512,512,1]{1,0,2:T(8,128)S(1)}, f32[512,512,1]{1,0,2:T(8,128)}, u32[]{:S(2)}) copy-start(f32[512,512,1]{1,0,2:T(8,128)} %convolution_bitcast_fusion.1) | copy-start | bytes 3145732
  406.5 44.5 %slice-start = ((s8[6291456]{0:T(1024)(128)(4,1)}), s8[2097152]{0:T(1024)(128)(4,1)S(1)}, s32[]{:S(2)}) async-start(s8[6291456]{0:T(1024)(128)(4,1)} %bitcast.155), calls=%async_computation.1 | async-start | bytes 4194304
  416.3 34.8 %slice-start.1 = ((s8[6291456]{0:T(1024)(128)(4,1)}), s8[4194304]{0:T(1024)(128)(4,1)S(1)}, s32[]{:S(2)}) async-start(s8[6291456]{0:T(1024)(128)(4,1)} %bitcast.155), calls=%async_computation.2 | async-start | bytes 8388608
  416.3 34.8 %copy-start = (f32[6,512,512]{2,0,1:T(8,128)S(1)}, f32[6,512,512]{2,0,1:T(8,128)}, u32[]{:S(2)}) copy-start(f32[6,512,512]{2,0,1:T(8,128)} %copy.69) | copy-start | bytes 18874372
  482.6 4.8 copy-start.7
  482.6 4.8 copy-start.13
  482.6 4.8 copy-start.16
  (14 other events, 19.6 us)
Sparse Core Ops, SparseCore 0:
  19.7 53.0 all-gather.2
where the time goes:
time: 589 us; the launch traced here: 581 us
  other arithmetic  193 us (33%)
  matrix products  182 us (31%)
  blocking collectives  103 us (17%)
  local copies, waits for them, and re-layouts  73.2 us (12%)
  between operations  19.7 us (3%)
  starting transfers between devices  9.73 us (2%)
    another operation x19, other arithmetic, fisher_terms(): factor = jnp.linalg.cholesky(cov)  121 us
    all_gather x1, blocking collectives, body(): lax.all_gather(coarse_coords, ('row', 'col'), axis=1, tiled=True)  65.1 us
    another operation x3, other arithmetic, fisher_terms(): inverse = jax.scipy.linalg.solve_triangular(factor, ident, lower=True)  51.7 us
    psum x1, blocking collectives, body(): grad, fisher = lax.psum((grad, fisher), ('row', 'col'))  38 us
    dot_general x1, matrix products, fisher_terms(): jnp.einsum('iab,jba->ij', joint_prod, joint_prod, precision=HIGH)  34.7 us
    dot_general x1, matrix products, fisher_terms(): joint_prod = jnp.einsum('ab,ibc->iac', joint_prec, derivs, precision=HIGH)  30.9 us
    dot_general x1, matrix products, score_terms(): jnp.einsum('rn,inm->irm', alpha, derivs, precision=HIGH) * alpha[None]  21.7 us
    dot_general x1, matrix products, fisher_terms(): lead_fish = jnp.einsum('iab,jba->ij', lead_prod, lead_prod, precision=HIGH)  18.9 us
  transfers between devices with their start and end apart: 5, of which 0 were waited for; matrix products, arithmetic and copies ran while one was open for 65% of the time, Pallas kernels for 0%

commit v1 on v0

v1 whole, which is shorter than its diff:
```python
import functools
import math

import jax
import jax.numpy as jnp
from jax import lax
from jax.experimental import pallas as pl
from jax.experimental.pallas import tpu as pltpu
from jax.sharding import PartitionSpec as P

HIGH = lax.Precision.HIGHEST
ROOT_FIVE = math.sqrt(5.0)
NUGGET = 0.2
RANGE_BASE = (0.5, 0.5, 0.5, 0.5)
BLK = 128
PAN = 16
F32 = jnp.float32


def mm(a, b):
    return jnp.dot(a, b, precision=HIGH, preferred_element_type=F32)


def mm_tn(a, b):
    return lax.dot_general(
        a, b, (((0,), (0,)), ((), ())), precision=HIGH, preferred_element_type=F32
    )


def rows(b):
    return pl.ds(b * BLK, BLK)


def inverse_factor(s_ref):
    row = lax.broadcasted_iota(jnp.int32, (PAN, BLK), 0)
    lane = lax.broadcasted_iota(jnp.int32, (PAN, BLK), 1)

    def panel(p, carry):
        start = pl.multiple_of(p * PAN, PAN)
        xa = s_ref[pl.ds(start, PAN), :BLK]
        xb = s_ref[pl.ds(start, PAN), BLK:]
        turned = pltpu.roll(xa, lax.rem(BLK - start, BLK), 1)
        cols = [jnp.broadcast_to(turned[:, j : j + 1], (PAN, BLK)) for j in range(PAN)]
        for k in range(PAN):
            inv = lax.rsqrt(cols[k][k : k + 1, :])
            low = cols[k] * inv
            for j in range(k + 1, PAN):
                cols[j] = cols[j] - low * low[j : j + 1, :]
            below = jnp.where(row > k, low, 0.0)
            ua = xa[k : k + 1, :] * inv
            ub = xb[k : k + 1, :] * inv
            xa = jnp.where(row == k, ua, xa - below * ua)
            xb = jnp.where(row == k, ub, xb - below * ub)
        s_ref[pl.ds(start, PAN), :BLK] = xa
        s_ref[pl.ds(start, PAN), BLK:] = xb
        tail = jnp.where(lane >= start + PAN, xa, 0.0)
        s_ref[...] -= mm_tn(tail, jnp.concatenate([xa, xb], axis=1))
        return carry

    lax.fori_loop(0, BLK // PAN, panel, 0)


def forward(u_ref, inv_ref, x_ref, count):
    for b in range(count):
        part = x_ref[rows(b), :]
        if b:
            part = part - mm_tn(u_ref[: b * BLK, b * BLK : (b + 1) * BLK], x_ref[: b * BLK, :])
        x_ref[rows(b), :] = mm(inv_ref[rows(b), :], part)


def model_kernel(reps, scal, xr, xc, u_ref, inv_ref, wt_ref, h_ref, z_ref, f_ref, c_ref, s_ref):
    n = xr.shape[1]
    nb = n // BLK
    lead = n - BLK
    lb = nb - 1
    variance, nugget = scal[0], scal[1]

    def cover(r, carry):
        start = pl.multiple_of(r * 64, 64)
        here = pl.ds(start, 64)
        total = None
        for k in range(4):
            diff = xc[here, k : k + 1] - xr[k : k + 1, :]
            total = diff * diff if total is None else total + diff * diff
        live_c = xc[here, 4:5]
        paired = live_c * xr[4:5, :]
        root = ROOT_FIVE * jnp.sqrt(total)
        decay = jnp.exp(-root) * (variance * paired)
        ident = (
            lax.broadcasted_iota(jnp.int32, (64, n), 0) + start
            == lax.broadcasted_iota(jnp.int32, (64, n), 1)
        )
        u_ref[here, :] = (1.0 + root + root * root / 3.0) * decay + jnp.where(
            ident, live_c * nugget + 1.0 - live_c, 0.0
        )
        c_ref[here, :] = (5.0 / 3.0) * (1.0 + root) * decay
        return carry

    lax.fori_loop(0, n // 64, cover, 0)

    eye = (
        lax.broadcasted_iota(jnp.int32, (BLK, BLK), 0)
        == lax.broadcasted_iota(jnp.int32, (BLK, BLK), 1)
    ).astype(F32)
    for b in range(nb):
        s_ref[:, :BLK] = u_ref[rows(b), b * BLK : (b + 1) * BLK]
        s_ref[:, BLK:] = eye
        inverse_factor(s_ref)
        inv = s_ref[:, BLK:]
        inv_ref[rows(b), :] = inv
        if b + 1 < nb:
            rest = (b + 1) * BLK
            u_ref[rows(b), rest:] = mm(inv, u_ref[rows(b), rest:])
            for i in range(b + 1, nb):
                u_ref[rows(i), i * BLK :] -= mm_tn(
                    u_ref[rows(b), i * BLK : (i + 1) * BLK], u_ref[rows(b), i * BLK :]
                )

    last = inv_ref[rows(lb), :]
    wt_ref[rows(lb), :] = last.T
    right = -mm(u_ref[:lead, lead:], last.T)
    for b in range(lb - 1, -1, -1):
        part = right[b * BLK : (b + 1) * BLK, :]
        if b + 1 < lb:
            part = part - mm(u_ref[rows(b), (b + 1) * BLK : lead], wt_ref[(b + 1) * BLK : lead, :])
        wt_ref[rows(b), :] = mm_tn(inv_ref[rows(b), :], part)

    wt = wt_ref[...]

    def slopes(r, carry):
        here = pl.ds(pl.multiple_of(r * BLK, BLK), BLK)
        for k in range(4):
            diff = xc[here, k : k + 1] - xr[k : k + 1, :]
            h_ref[here, k * BLK : (k + 1) * BLK] = mm(c_ref[here, :] * (diff * diff), wt)
        h_ref[here, 4 * BLK :] = nugget * wt_ref[here, :]
        return carry

    lax.fori_loop(0, nb, slopes, 0)
    z_ref[...] = mm_tn(wt, h_ref[...])
    forward(u_ref, inv_ref, h_ref, lb)

    def h_of(i):
        i = 4 if i in (0, 5) else i - 1
        return h_ref[:lead, i * BLK : (i + 1) * BLK]

    def z_of(i):
        if i == 0:
            return eye - z_ref[:, 4 * BLK :]
        return z_ref[:, (i - 1) * BLK : i * BLK]

    row8 = lax.broadcasted_iota(jnp.int32, (8, BLK), 0)
    lane8 = lax.broadcasted_iota(jnp.int32, (8, BLK), 1)
    out = jnp.zeros((8, BLK), F32)
    for i in range(6):
        for j in range(i, 6):
            sign = -2.0 if (i == 0) != (j == 0) else 2.0
            both = sign * jnp.sum(h_of(i) * h_of(j), axis=0, keepdims=True)
            both = both + jnp.sum(z_of(i) * z_of(j), axis=0, keepdims=True)
            value = (0.5 * reps) * jnp.sum(both, axis=1, keepdims=True)
            spot = (row8 == i) & (lane8 == j) | (row8 == j) & (lane8 == i)
            out = out + jnp.where(spot, value, 0.0)
    f_ref[...] = out


def data_kernel(
    coarse, upper, left, own, cidx, fidx, u_ref, inv_ref, wt_ref, h_ref, z_ref, f_ref,
    white_ref, out_ref, m_ref,
):
    reps = own.shape[0]
    n = wt_ref.shape[0]
    lead = n - BLK
    nc = cidx.shape[1]
    half = fidx.shape[1] // 2

    def onehot(index, count):
        return (
            lax.broadcasted_iota(jnp.int32, (count, index.shape[1]), 0) == index
        ).astype(F32)

    hot_c = onehot(cidx[...], coarse.shape[1])
    hot_u = onehot(fidx[:, :half], upper.shape[1])
    hot_l = onehot(fidx[:, half:], left.shape[1])
    white = mm(coarse[...], mm(hot_c, wt_ref[:nc, :]))
    white = white + mm(upper[...], mm(hot_u, wt_ref[nc : nc + half, :]))
    white = white + mm(left[...], mm(hot_l, wt_ref[nc + half : lead, :]))
    white = white + mm(own[...], wt_ref[lead:, :])
    white_ref[...] = white
    m_ref[:nc, :] = mm_tn(hot_c, mm_tn(coarse[...], white))
    m_ref[nc : nc + half, :] = mm_tn(hot_u, mm_tn(upper[...], white))
    m_ref[nc + half :, :] = mm_tn(hot_l, mm_tn(left[...], white))
    forward(u_ref, inv_ref, m_ref, lead // BLK)
    gram = mm_tn(white, white)
    eye = (
        lax.broadcasted_iota(jnp.int32, (BLK, BLK), 0)
        == lax.broadcasted_iota(jnp.int32, (BLK, BLK), 1)
    ).astype(F32)
    weight = 0.5 * gram - (0.5 * reps) * eye
    row8 = lax.broadcasted_iota(jnp.int32, (8, BLK), 0)
    lane8 = lax.broadcasted_iota(jnp.int32, (8, BLK), 1)
    out = f_ref[...]
    for i in range(6):
        at = 4 if i in (0, 5) else i - 1
        lead_part = jnp.sum(m_ref[...] * h_ref[:lead, at * BLK : (at + 1) * BLK], axis=0, keepdims=True)
        z = z_ref[:, at * BLK : (at + 1) * BLK]
        if i == 0:
            z = eye - z
            lead_part = -lead_part
        both = lead_part + jnp.sum(weight * z, axis=0, keepdims=True)
        value = jnp.sum(both, axis=1, keepdims=True)
        out = out + jnp.where((row8 == i) & (lane8 == 6), value, 0.0)
    out_ref[...] = out


def solve_kernel(x_ref, out_ref):
    out_ref[...] = eliminated(x_ref[...])


def eliminated(x):
    row8 = lax.broadcasted_iota(jnp.int32, (8, BLK), 0)
    for k in range(6):
        top = x[k : k + 1, :] / x[k : k + 1, k : k + 1]
        x = jnp.where(row8 == k, top, x - x[:, k : k + 1] * top)
    return x


def vmem(count):
    return [pl.BlockSpec(memory_space=pltpu.VMEM)] * count


def shape(*dims):
    return jax.ShapeDtypeStruct(dims, F32)


def body(coords, values, coarse_coords, coarse_values, fine_index, coarse_index, log_params):
    half = fine_index.shape[1] // 2
    reps = values.shape[0]
    block = coords.shape[1]
    nc = coarse_index.shape[1]
    n = nc + 2 * half + block
    n_row, n_col = lax.axis_size("row"), lax.axis_size("col")
    down = [(i, i + 1) for i in range(n_row - 1)]
    across = [((i - 1) % n_col, i) for i in range(n_col)]
    all_coords = lax.all_gather(coarse_coords, ("row", "col"), axis=1, tiled=True)
    upper_coords = lax.ppermute(coords, "row", down)
    left_coords = lax.ppermute(coords, "col", across)
    upper_values = lax.ppermute(values, "row", down)
    left_values = lax.ppermute(values, "col", across)
    all_values = lax.all_gather(coarse_values, ("row", "col"), axis=1, tiled=True)

    def pick(array, index):
        hot = (index[None, :] == jnp.arange(array.shape[1], dtype=jnp.int32)[:, None]).astype(F32)
        return jnp.dot(array, hot, precision=HIGH)

    upper_live = (lax.axis_index("row") > 0).astype(F32)
    joint = jnp.concatenate(
        [
            pick(all_coords, coarse_index[0]),
            pick(upper_coords, fine_index[0, :half]),
            pick(left_coords, fine_index[0, half:]),
            coords,
        ],
        axis=1,
    )
    scale = jnp.exp(log_params[1:5]) * jnp.array(RANGE_BASE, F32)
    live = jnp.concatenate(
        [jnp.ones((nc,), F32), upper_live * jnp.ones((half,), F32), jnp.ones((half + block,), F32)]
    )
    xr = jnp.concatenate([joint / scale[:, None], live[None], jnp.zeros((3, n), F32)], axis=0)
    scal = jnp.stack([jnp.exp(log_params[0]), NUGGET * jnp.exp(log_params[5])])
    lead = n - block
    u, inv, wt, h, z, fish = pl.pallas_call(
        functools.partial(model_kernel, float(reps)),
        out_shape=[
            shape(n, n), shape(n, BLK), shape(n, BLK), shape(n, 5 * BLK), shape(BLK, 5 * BLK),
            shape(8, BLK),
        ],
        in_specs=[pl.BlockSpec(memory_space=pltpu.SMEM)] + vmem(2),
        out_specs=vmem(6),
        scratch_shapes=[pltpu.VMEM((n, n), F32), pltpu.VMEM((BLK, 2 * BLK), F32)],
        compiler_params=pltpu.CompilerParams(vmem_limit_bytes=40 * 1024 * 1024),
        cost_estimate=pl.CostEstimate(
            flops=60_000_000_000, bytes_accessed=8_000_000, transcendentals=2 * n * n
        ),
    )(scal, xr, xr.T)
    white, terms = pl.pallas_call(
        data_kernel,
        out_shape=[shape(reps, BLK), shape(8, BLK)],
        in_specs=vmem(12),
        out_specs=vmem(2),
        scratch_shapes=[pltpu.VMEM((lead, BLK), F32)],
        compiler_params=pltpu.CompilerParams(vmem_limit_bytes=40 * 1024 * 1024),
    )(all_values, upper_values, left_values, values, coarse_index, fine_index, u, inv, wt, h, z, fish)
    total = lax.psum(terms, ("row", "col"))
    solved = pl.pallas_call(
        solve_kernel, out_shape=shape(8, BLK), in_specs=vmem(1), out_specs=vmem(1)[0]
    )(total)
    return (solved[:6, 6], white)


def solution(mesh):
    in_specs = (
        P(None, ("row", "col")),
        P(None, ("row", "col")),
        P(None, ("row", "col")),
        P(None, ("row", "col")),
        P(("row", "col"), None),
        P(("row", "col"), None),
        P(),
    )
    out_specs = (P(), P(None, ("row", "col")))
    return jax.shard_map(body, mesh=mesh, in_specs=in_specs, out_specs=out_specs, check_vma=False)
```

time: 589 us -> 200 us (0.34); the launches traced: 581 us -> 199 us
  other arithmetic: 193 us -> 2.45 us
  matrix products: 182 us -> 0.62 us
  local copies, waits for them, and re-layouts: 73.2 us -> 10.7 us
  Pallas kernels: 0 us -> 56.2 us
    another operation x27 -> x1, other arithmetic: 175 us -> 0.07 us  [body(): scal = jnp.stack([jnp.exp(log_params[0]), NUGGET * jnp.exp(log_params[5])])]
    dot_general x13 -> x3, matrix products: 163 us -> 0.62 us  [pick(): return jnp.dot(array, hot, precision=HIGH)]
    pallas_call x0 -> x3, Pallas kernels: none -> 56.2 us  [the longest x1 44.7 us: body(): pl.pallas_call(functools.partial(model_kernel, float(reps)), out_shape=[s...]
    transpose x2 -> x0, local copies, waits for them, and re-layouts: 24.2 us -> none  [the longest x1 14.5 us: fisher_terms(): joint_prod = jnp.einsum('ab,ibc->iac', joint_prec, derivs, precision=HIGH)]
    another operation x19 -> x0, matrix products: 18.7 us -> none  [the longest x9 10.8 us: fisher_terms(): inverse = jax.scipy.linalg.solve_triangular(factor, ident, lower=True)]
    another operation x21 -> x0, local copies, waits for them, and re-layouts: 15.9 us -> none
    mul x5 -> x1, local copies, waits for them, and re-layouts: 9.85 us -> 0.01 us  [body(): upper_live * jnp.ones((half,), F32)]
    mul x5 -> x1, other arithmetic: 8.63 us -> 0.73 us  [body(): scale = jnp.exp(log_params[1:5]) * jnp.array(RANGE_BASE, F32)]
  transfers between devices with their start and end apart: 5 -> 5, of which waited for: 0 -> 0; matrix products, arithmetic and copies ran while one was open for 65% -> 4% of each run, Pallas kernels for 0% -> 23%
where the time goes in v1:
time: 200 us; the launch traced here: 199 us
  blocking collectives  103 us (52%)
  Pallas kernels  56.2 us (28%)
  between operations  15.5 us (8%)
  local copies, waits for them, and re-layouts  10.7 us (5%)
  starting transfers between devices  10.4 us (5%)
  other arithmetic  2.45 us (1%)
    all_gather x1, blocking collectives, body(): lax.all_gather(coarse_coords, ('row', 'col'), axis=1, tiled=True)  65.4 us
    pallas_call x1, Pallas kernels, body(): pl.pallas_call(functools.partial(model_kernel, float(reps)), out_shape=[s...  44.7 us
    psum x1, blocking collectives, body(): total = lax.psum(terms, ('row', 'col'))  37.2 us
    pallas_call x1, Pallas kernels, body(): pl.pallas_call(data_kernel, out_shape=[shape(reps, BLK), shape(8, BLK)],...  9.76 us
    unnamed x15, local copies, waits for them, and re-layouts  5.37 us
    ppermute x1, starting transfers between devices, body(): upper_values = lax.ppermute(values, 'row', down)  4.1 us
  transfers between devices with their start and end apart: 5, of which 0 were waited for; matrix products, arithmetic and copies ran while one was open for 4% of the time, Pallas kernels for 23%

profile of v1, /device:TPU:0, one launch (start us, length us, event | category | flops | bytes accessed | tf_op | source)
XLA Modules:
  0.0 198.5 jit_solution(11266309914519072550)
XLA Ops:
  7.2 0.0 all-gather.3.cloned.1.call-start
  7.2 2.4 %collective-permute-start.2 = (f32[4,128]{1,0:T(4,128)}, f32[4,128]{1,0:T(4,128)S(1)}, u32[]{:S(2)}, u32[]{:S(2)}) collective-permute-start(f32[4,128]{1,0:T(4,128)} %param.8), channel_id=1, source_target_pairs={{0,8},{8,16},{16,24},{1,9},{9,17},{17,25},{2,10},{10,18},{18,26},{... | collective-permute-start | bytes 6152 | tf_op jit(solution)/shard_map/ppermute | solution.py:244
  9.6 2.4 %collective-permute-start.3 = (f32[4,128]{1,0:T(4,128)}, f32[4,128]{1,0:T(4,128)S(1)}, u32[]{:S(2)}, u32[]{:S(2)}) collective-permute-start(f32[4,128]{1,0:T(4,128)} %param.8), channel_id=1, source_target_pairs={{7,0},{0,1},{1,2},{2,3},{3,4},{4,5},{5,6},{6,7},{15,8},{8,9},{9,10... | collective-permute-start | bytes 6152 | tf_op jit(solution)/shard_map/ppermute | solution.py:245
  12.0 4.1 %collective-permute-start = (f32[512,128]{1,0:T(8,128)}, f32[512,128]{1,0:T(8,128)}, u32[]{:S(2)}, u32[]{:S(2)}) collective-permute-start(f32[512,128]{1,0:T(8,128)} %own.1), channel_id=1, source_target_pairs={{0,8},{8,16},{16,24},{1,9},{9,17},{17,25},{2,10},{10,18},{18,26},{... | collective-permute-start | bytes 786440 | tf_op jit(solution)/shard_map/ppermute | solution.py:246
  16.1 1.5 collective-permute-start.1
  17.6 0.0 all-gather.3.cloned.1.call-update
  17.7 0.7 exponential_multiply_fusion
  18.4 1.3 fusion.3
  19.7 0.8 slice_bitcast_fusion.1
  21.9 0.7 reduce
  22.6 65.4 %all-gather = f32[32,16,4]{1,2,0:T(4,128)S(1)} all-gather(f32[1,16,4]{1,2,0:T(4,128)} %bitcast.20), channel_id=1, replica_groups=mesh['row'=4,'col'=8] {'row','col'}, dimensions={0}, use_global_device_ids=true | all-gather | bytes 8448 | tf_op jit(solution)/shard_map/all_gather | solution.py:243
  88.0 0.1 reshape.12
  88.1 0.3 convolution_bitcast_fusion
  88.4 0.1 pad_maximum_fusion
  88.5 0.1 pad_maximum_fusion.1.scal
  88.6 0.1 pad.2.clone
  88.7 0.1 convolution_bitcast_fusion.2
  88.8 0.2 convolution_bitcast_fusion.1
  88.9 0.8 maximum_divide_fusion
  89.7 0.1 maximum_maximum_fusion.xr
  89.8 0.2 copy.25
  90.0 44.7 %shard_map.95 = (f32[640,640]{1,0:T(8,128)S(1)}, f32[640,128]{1,0:T(8,128)S(1)}, f32[640,128]{1,0:T(8,128)S(1)}, f32[640,640]{1,0:T(8,128)S(1)}, f32[128,640]{1,0:T(8,128)S(1)}, /*index=5*/f32[8,128]{1,0:T(8,128)S(1)}) custom-call(f32[2]{0:T(128)S(1)} %pad_maximum_fusion.1.scal, f32[8,640]{1,0:T(8,128)S(1)} %maximum_maximum_fusion.xr, f32[640,8]{1,0:T(8,128)S(1)} %bitcast.19), custom_call_target="tpu_custom_call" | custom-call | flops 60000002048 | bytes 8000000 | tf_op jit(solution)/shard_map/pallas_call | solution.py:271
  134.7 1.2 copy-done
  135.9 0.7 copy-done.2
  136.7 1.6 copy.26.coarse
  138.3 1.4 copy-done.1
  139.7 1.0 copy-done.3
  140.7 0.9 copy-done.4
  141.6 9.8 %shard_map.96 = (f32[512,128]{1,0:T(8,128)}, f32[8,128]{1,0:T(8,128)S(1)}) custom-call(f32[512,512]{1,0:T(8,128)S(1)} %copy.26.coarse, f32[512,128]{1,0:T(8,128)} %collective-permute-done.upper, f32[512,128]{1,0:T(8,128)} %collective-permute-done.1.left, f32[512,128]{1,0:T(8,128)S(1)} %copy-done.4, s32[1,384]{1,0:T(1,128)S(1)} %copy-done.5, ...), custom_call_target="tpu_custom_call" | custom-call | tf_op jit(solution)/shard_map/pallas_call | solution.py:285
  151.4 37.2 %psum.7.x_ref = f32[8,128]{1,0:T(8,128)} all-reduce(f32[8,128]{1,0:T(8,128)S(1)} %get-tuple-element.16), channel_id=1, replica_groups=mesh['row'=4,'col'=8] {'row','col'}, use_global_device_ids=true, to_apply=%region_0.0 | all-reduce | flops 1024 | bytes 8192 | tf_op jit(solution)/shard_map/psum | solution.py:293
  188.6 1.7 shard_map.97
  190.3 1.4 slice_reduce_fusion
  (20 shorter events, 0.0 us)
Async XLA Ops:
  7.2 129.5 %all-gather.3.cloned.1.call-start = ((), (), s32[]{:S(2)}) async-start(), calls=%async_computation | async-start | bytes 1081344 | tf_op jit(solution)/shard_map/all_gather | solution.py:248
  7.2 81.5 %collective-permute-start.2 = (f32[4,128]{1,0:T(4,128)}, f32[4,128]{1,0:T(4,128)S(1)}, u32[]{:S(2)}, u32[]{:S(2)}) collective-permute-start(f32[4,128]{1,0:T(4,128)} %param.8), channel_id=1, source_target_pairs={{0,8},{8,16},{16,24},{1,9},{9,17},{17,25},{2,10},{10,18},{18,26},{... | collective-permute-start | bytes 6152 | tf_op jit(solution)/shard_map/ppermute | solution.py:244
  9.6 79.2 %collective-permute-start.3 = (f32[4,128]{1,0:T(4,128)}, f32[4,128]{1,0:T(4,128)S(1)}, u32[]{:S(2)}, u32[]{:S(2)}) collective-permute-start(f32[4,128]{1,0:T(4,128)} %param.8), channel_id=1, source_target_pairs={{7,0},{0,1},{1,2},{2,3},{3,4},{4,5},{5,6},{6,7},{15,8},{8,9},{9,10... | collective-permute-start | bytes 6152 | tf_op jit(solution)/shard_map/ppermute | solution.py:245
  12.0 126.2 %collective-permute-start = (f32[512,128]{1,0:T(8,128)}, f32[512,128]{1,0:T(8,128)}, u32[]{:S(2)}, u32[]{:S(2)}) collective-permute-start(f32[512,128]{1,0:T(8,128)} %own.1), channel_id=1, source_target_pairs={{0,8},{8,16},{16,24},{1,9},{9,17},{17,25},{2,10},{10,18},{18,26},{... | collective-permute-start | bytes 786440 | tf_op jit(solution)/shard_map/ppermute | solution.py:246
  16.1 122.2 %collective-permute-start.1 = (f32[512,128]{1,0:T(8,128)}, f32[512,128]{1,0:T(8,128)}, u32[]{:S(2)}, u32[]{:S(2)}) collective-permute-start(f32[512,128]{1,0:T(8,128)} %own.1), channel_id=1, source_target_pairs={{7,0},{0,1},{1,2},{2,3},{3,4},{4,5},{5,6},{6,7},{15,8},{8,9},{9,10... | collective-permute-start | bytes 786440 | tf_op jit(solution)/shard_map/ppermute | solution.py:247
  134.7 1.2 copy-start
  135.9 0.7 copy-start.2
  136.6 1.6 copy-start.5
  136.7 1.6 copy-start.6
  138.3 1.4 copy-start.1
  139.7 1.0 copy-start.3
  140.7 0.9 copy-start.4
Sparse Core Ops, SparseCore 0:
  17.8 53.0 all-gather.2

commit v2 on v1

--- a/solution.py
+++ b/solution.py
@@ -68,12 +68,44 @@
         x_ref[rows(b), :] = mm(inv_ref[rows(b), :], part)
 
 
-def model_kernel(reps, scal, xr, xc, u_ref, inv_ref, wt_ref, h_ref, z_ref, f_ref, c_ref, s_ref):
+def model_kernel(
+    reps, per_tile, scal, where, held, cidx, fidx, u_ref, inv_ref, wt_ref, h_ref, z_ref, f_ref,
+    c_ref, s_ref, xr, xc,
+):
     n = xr.shape[1]
     nb = n // BLK
     lead = n - BLK
     lb = nb - 1
+    nc = cidx.shape[1]
+    half = fidx.shape[1] // 2
+    count = held.shape[0]
     variance, nugget = scal[0], scal[1]
+    row8 = lax.broadcasted_iota(jnp.int32, (8, BLK), 0)
+    scale = sum(jnp.where(row8 == k, scal[2 + k], 0.0) for k in range(4))[:, :1]
+
+    wanted = cidx[...]
+    tile = wanted // per_tile
+    spot = wanted - tile * per_tile
+    hot = (lax.broadcasted_iota(jnp.int32, (BLK, nc), 0) == spot).astype(F32)
+    spread = mm(held[...].reshape(count * 8, BLK), hot).reshape(count, 8, nc)
+    owner = lax.broadcasted_iota(jnp.int32, (count, 8, nc), 0)
+    coarse = jnp.sum(jnp.where(owner == tile[None], spread, 0.0), axis=0)
+    xr[:, :nc] = pltpu.roll(coarse, 4, 0) * scale
+
+    def neighbour(device, index):
+        pick = (lax.broadcasted_iota(jnp.int32, (BLK, half), 0) == index).astype(F32)
+        return mm(held[device], pick) * scale
+
+    alive = jnp.where(where[1] > 0, 1.0, 0.0)
+    near = jnp.concatenate(
+        [neighbour(where[2], fidx[:, :half]) * alive, neighbour(where[3], fidx[:, half:])], axis=1
+    )
+    xr[:, nc:lead] = near
+    xr[:, lead:] = held[where[0]] * scale
+    point = lax.broadcasted_iota(jnp.int32, (1, n), 1)
+    xr[4:5, :] = jnp.where((point >= nc) & (point < nc + half), alive, 1.0)
+    for b in range(nb):
+        xc[rows(b), :] = xr[:, b * BLK : (b + 1) * BLK].T
 
     def cover(r, carry):
         start = pl.multiple_of(r * 64, 64)
@@ -148,7 +180,6 @@
             return eye - z_ref[:, 4 * BLK :]
         return z_ref[:, (i - 1) * BLK : i * BLK]
 
-    row8 = lax.broadcasted_iota(jnp.int32, (8, BLK), 0)
     lane8 = lax.broadcasted_iota(jnp.int32, (8, BLK), 1)
     out = jnp.zeros((8, BLK), F32)
     for i in range(6):
@@ -211,8 +242,70 @@
     out_ref[...] = out
 
 
-def solve_kernel(x_ref, out_ref):
-    out_ref[...] = eliminated(x_ref[...])
+def exchange(x_ref, held, send_sem, recv_sem):
+    n_row, n_col = lax.axis_size("row"), lax.axis_size("col")
+    count = n_row * n_col
+    me = lax.axis_index("row") * n_col + lax.axis_index("col")
+
+    def place(device):
+        return {"row": device // n_col, "col": lax.rem(device, n_col)}
+
+    barrier = pltpu.get_barrier_semaphore()
+
+    def greet(d, carry):
+        pl.semaphore_signal(
+            barrier, inc=1, device_id=place(lax.rem(me + d, count)),
+            device_id_type=pl.DeviceIdType.MESH,
+        )
+        return carry
+
+    lax.fori_loop(1, count, greet, 0)
+    pl.semaphore_wait(barrier, count - 1)
+
+    def copy(d, slot):
+        return pltpu.make_async_remote_copy(
+            src_ref=x_ref, dst_ref=held.at[slot], send_sem=send_sem.at[d],
+            recv_sem=recv_sem.at[d], device_id=place(lax.rem(me + d, count)),
+            device_id_type=pl.DeviceIdType.MESH,
+        )
+
+    def push(d, carry):
+        copy(d, me).start()
+        return carry
+
+    def settle(d, carry):
+        copy(d, lax.rem(me - d + count, count)).wait()
+        return carry
+
+    lax.fori_loop(1, count, push, 0)
+    held[me] = x_ref[...]
+    lax.fori_loop(1, count, settle, 0)
+
+
+def share_kernel(x_ref, out_ref, held, send_sem, recv_sem):
+    exchange(x_ref, held, send_sem, recv_sem)
+    out_ref[...] = held[...]
+
+
+def solve_kernel(x_ref, out_ref, held, send_sem, recv_sem):
+    exchange(x_ref, held, send_sem, recv_sem)
+    out_ref[...] = eliminated(jnp.sum(held[...], axis=0))
+
+
+def exchanged(kernel, out_shape, number, payload):
+    count = lax.axis_size("row") * lax.axis_size("col")
+    return pl.pallas_call(
+        kernel,
+        out_shape=out_shape,
+        in_specs=vmem(1),
+        out_specs=vmem(1)[0],
+        scratch_shapes=[
+            pltpu.VMEM((count, 8, BLK), F32),
+            pltpu.SemaphoreType.DMA((count,)),
+            pltpu.SemaphoreType.DMA((count,)),
+        ],
+        compiler_params=pltpu.CompilerParams(collective_id=number, has_side_effects=True),
+    )(payload)
 
 
 def eliminated(x):
@@ -240,48 +333,44 @@
     n_row, n_col = lax.axis_size("row"), lax.axis_size("col")
     down = [(i, i + 1) for i in range(n_row - 1)]
     across = [((i - 1) % n_col, i) for i in range(n_col)]
-    all_coords = lax.all_gather(coarse_coords, ("row", "col"), axis=1, tiled=True)
-    upper_coords = lax.ppermute(coords, "row", down)
-    left_coords = lax.ppermute(coords, "col", across)
+    payload = jnp.concatenate(
+        [coords, jnp.pad(coarse_coords, ((0, 0), (0, block - coarse_coords.shape[1])))], axis=0
+    )
+    held = exchanged(share_kernel, shape(n_row * n_col, 8, BLK), 0, payload)
     upper_values = lax.ppermute(values, "row", down)
     left_values = lax.ppermute(values, "col", across)
     all_values = lax.all_gather(coarse_values, ("row", "col"), axis=1, tiled=True)
-
-    def pick(array, index):
-        hot = (index[None, :] == jnp.arange(array.shape[1], dtype=jnp.int32)[:, None]).astype(F32)
-        return jnp.dot(array, hot, precision=HIGH)
-
-    upper_live = (lax.axis_index("row") > 0).astype(F32)
-    joint = jnp.concatenate(
+    scale = jnp.exp(log_params[1:5]) * jnp.array(RANGE_BASE, F32)
+    scal = jnp.concatenate(
+        [jnp.exp(log_params[:1]), NUGGET * jnp.exp(log_params[5:]), 1.0 / scale]
+    )
+    row, col = lax.axis_index("row"), lax.axis_index("col")
+    where = jnp.stack(
         [
-            pick(all_coords, coarse_index[0]),
-            pick(upper_coords, fine_index[0, :half]),
-            pick(left_coords, fine_index[0, half:]),
-            coords,
-        ],
-        axis=1,
-    )
-    scale = jnp.exp(log_params[1:5]) * jnp.array(RANGE_BASE, F32)
-    live = jnp.concatenate(
-        [jnp.ones((nc,), F32), upper_live * jnp.ones((half,), F32), jnp.ones((half + block,), F32)]
-    )
-    xr = jnp.concatenate([joint / scale[:, None], live[None], jnp.zeros((3, n), F32)], axis=0)
-    scal = jnp.stack([jnp.exp(log_params[0]), NUGGET * jnp.exp(log_params[5])])
+            row * n_col + col,
+            row,
+            jnp.maximum(row - 1, 0) * n_col + col,
+            row * n_col + lax.rem(col + n_col - 1, n_col),
+        ]
+    ).astype(jnp.int32)
     lead = n - block
     u, inv, wt, h, z, fish = pl.pallas_call(
-        functools.partial(model_kernel, float(reps)),
+        functools.partial(model_kernel, float(reps), coarse_coords.shape[1]),
         out_shape=[
             shape(n, n), shape(n, BLK), shape(n, BLK), shape(n, 5 * BLK), shape(BLK, 5 * BLK),
             shape(8, BLK),
         ],
-        in_specs=[pl.BlockSpec(memory_space=pltpu.SMEM)] + vmem(2),
+        in_specs=[pl.BlockSpec(memory_space=pltpu.SMEM)] * 2 + vmem(3),
         out_specs=vmem(6),
-        scratch_shapes=[pltpu.VMEM((n, n), F32), pltpu.VMEM((BLK, 2 * BLK), F32)],
+        scratch_shapes=[
+            pltpu.VMEM((n, n), F32), pltpu.VMEM((BLK, 2 * BLK), F32),
+            pltpu.VMEM((8, n), F32), pltpu.VMEM((n, 8), F32),
+        ],
         compiler_params=pltpu.CompilerParams(vmem_limit_bytes=40 * 1024 * 1024),
         cost_estimate=pl.CostEstimate(
             flops=60_000_000_000, bytes_accessed=8_000_000, transcendentals=2 * n * n
         ),
-    )(scal, xr, xr.T)
+    )(scal, where, held, coarse_index, fine_index)
     white, terms = pl.pallas_call(
         data_kernel,
         out_shape=[shape(reps, BLK), shape(8, BLK)],
@@ -290,10 +379,7 @@
         scratch_shapes=[pltpu.VMEM((lead, BLK), F32)],
         compiler_params=pltpu.CompilerParams(vmem_limit_bytes=40 * 1024 * 1024),
     )(all_values, upper_values, left_values, values, coarse_index, fine_index, u, inv, wt, h, z, fish)
-    total = lax.psum(terms, ("row", "col"))
-    solved = pl.pallas_call(
-        solve_kernel, out_shape=shape(8, BLK), in_specs=vmem(1), out_specs=vmem(1)[0]
-    )(total)
+    solved = exchanged(solve_kernel, shape(8, BLK), 1, terms)
     return (solved[:6, 6], white)
 
 

time: 200 us -> 114 us (0.57)
  blocking collectives: 103 us -> 0 us
  Pallas kernels: 56.2 us -> 77.7 us
  starting transfers between devices: 10.4 us -> 5.49 us
    all_gather x1 -> x0, blocking collectives: 65.4 us -> none  [body(): lax.all_gather(coarse_coords, ('row', 'col'), axis=1, tiled=True)]
    psum x1 -> x0, blocking collectives: 37.2 us -> none  [body(): total = lax.psum(terms, ('row', 'col'))]
    pallas_call x2 -> x3, Pallas kernels: 46.5 us -> 68 us  [the longest x1 45.6 us: body(): pl.pallas_call(functools.partial(model_kernel, float(reps), coarse_coords...]
    ppermute x2 -> x0, starting transfers between devices: 4.79 us -> none  [the longest x1 2.4 us: body(): upper_coords = lax.ppermute(coords, 'row', down)]
    unnamed x15 -> x22, local copies, waits for them, and re-layouts: 5.37 us -> 8.11 us
  transfers between devices with their start and end apart: 5 -> 3, of which waited for: 0 -> 0; matrix products, arithmetic and copies ran while one was open for 4% -> 4% of each run, Pallas kernels for 23% -> 50%
where the time goes in v2:
time: 114 us; the launch traced here: 113 us
  Pallas kernels  77.7 us (68%)
  between operations  15.5 us (14%)
  local copies, waits for them, and re-layouts  12.4 us (11%)
  starting transfers between devices  5.49 us (5%)
  other arithmetic  2.19 us (2%)
    pallas_call x1, Pallas kernels, body(): pl.pallas_call(functools.partial(model_kernel, float(reps), coarse_coords...  45.6 us
    pallas_call x2, Pallas kernels, exchanged(): pl.pallas_call(kernel, out_shape=out_shape, in_specs=vmem(1), out_specs=v...  22.4 us
    pallas_call x1, Pallas kernels, body(): pl.pallas_call(data_kernel, out_shape=[shape(reps, BLK), shape(8, BLK)],...  9.75 us
    unnamed x22, local copies, waits for them, and re-layouts  8.11 us
    ppermute x1, starting transfers between devices, body(): upper_values = lax.ppermute(values, 'row', down)  3.12 us
    ppermute x1, starting transfers between devices, body(): left_values = lax.ppermute(values, 'col', across)  2.34 us
  transfers between devices with their start and end apart: 3, of which 0 were waited for; matrix products, arithmetic and copies ran while one was open for 4% of the time, Pallas kernels for 50%

profile of v2, /device:TPU:0, one launch (start us, length us, event | category | flops | bytes accessed | tf_op | source)
XLA Modules:
  0.0 113.3 jit_solution(7430843342748247271)
XLA Ops:
  7.2 0.0 all-gather.2.cloned.1.call-start
  7.2 3.1 %collective-permute-start = (f32[512,128]{1,0:T(8,128)}, f32[512,128]{1,0:T(8,128)}, u32[]{:S(2)}, u32[]{:S(2)}) collective-permute-start(f32[512,128]{1,0:T(8,128)} %own.1), channel_id=1, source_target_pairs={{0,8},{8,16},{16,24},{1,9},{9,17},{17,25},{2,10},{10,18},{18,26},{... | collective-permute-start | bytes 786440 | tf_op jit(solution)/shard_map/ppermute | solution.py:340
  10.3 2.3 %collective-permute-start.1 = (f32[512,128]{1,0:T(8,128)}, f32[512,128]{1,0:T(8,128)}, u32[]{:S(2)}, u32[]{:S(2)}) collective-permute-start(f32[512,128]{1,0:T(8,128)} %own.1), channel_id=1, source_target_pairs={{7,0},{0,1},{1,2},{2,3},{3,4},{4,5},{5,6},{6,7},{15,8},{8,9},{9,10... | collective-permute-start | bytes 786440 | tf_op jit(solution)/shard_map/ppermute | solution.py:341
  12.7 0.0 all-gather.2.cloned.1.call-update
  12.7 0.7 multiply_divide_fusion
  13.4 1.3 %fusion = (f32[1]{0:T(128)}, f32[1]{0:T(128)}) fusion(f32[6]{0:T(128)} %param.14), kind=kLoop, calls=%fused_computation.6 | loop fusion | bytes 16 | tf_op jit(solution)/shard_map/slice | solution.py:345
  16.1 1.3 %select_maximum_fusion.x_ref = f32[8,128]{1,0:T(8,128)} fusion(f32[4,16]{1,0:T(4,128)} %param.10, f32[4,128]{1,0:T(4,128)} %param.8), kind=kLoop, calls=%fused_computation | loop fusion | flops 3072 | bytes 6400 | tf_op jit(solution)/shard_map/concatenate | solution.py:336
  17.4 11.3 %shard_map.95.held = f32[32,8,128]{2,1,0:T(8,128)} custom-call(f32[8,128]{1,0:T(8,128)} %select_maximum_fusion.x_ref), custom_call_target="tpu_custom_call" | custom-call | tf_op jit(solution)/shard_map/pallas_call | solution.py:297
  28.7 0.1 pad_maximum_fusion.scal
  28.8 0.1 pad_add_fusion.where
  28.9 0.0 copy-start.5
  28.9 0.9 copy-done.5
  29.8 0.0 copy-start.7
  29.8 0.7 copy-done.7
  30.5 0.7 copy-done.9
  31.1 45.6 %shard_map.96 = (f32[640,640]{1,0:T(8,128)S(1)}, f32[640,128]{1,0:T(8,128)S(1)}, f32[640,128]{1,0:T(8,128)S(1)}, f32[640,640]{1,0:T(8,128)S(1)}, f32[128,640]{1,0:T(8,128)S(1)}, /*index=5*/f32[8,128]{1,0:T(8,128)S(1)}) custom-call(f32[6]{0:T(128)S(1)} %pad_maximum_fusion.scal, s32[4]{0:T(128)S(1)} %pad_add_fusion.where, f32[32,8,128]{2,1,0:T(8,128)S(1)} %copy-done.5, ...), custom_call_target="tpu_custom_call" | custom-call | flops 60000002048 | bytes 8000000 | tf_op jit(solution)/shard_map/pallas_call | solution.py:357
  76.7 0.0 copy-start
  76.7 1.2 %copy-done = f32[640,640]{1,0:T(8,128)} copy-done((f32[640,640]{1,0:T(8,128)}, f32[640,640]{1,0:T(8,128)S(1)}, u32[]{:S(2)}) %copy-start) | copy-done | bytes 1638424
  77.9 0.7 copy-done.2
  78.7 1.6 %copy.12.coarse = f32[512,512]{1,0:T(8,128)S(1)} copy(f32[512,512]{0,1:T(8,128)} %all-gather.2.cloned.1.call-done) | data formatting | bytes 2097152 | tf_op jit(solution)/shard_map/all_gather | solution.py:342
  80.2 0.0 collective-permute-done.upper
  80.3 0.0 collective-permute-done.1.left
  80.3 0.0 copy-done.8
  80.3 0.0 copy-done.10
  80.3 0.0 copy-start.1
  80.3 1.4 %copy-done.1 = f32[640,640]{1,0:T(8,128)S(1)} copy-done((f32[640,640]{1,0:T(8,128)S(1)}, f32[640,640]{1,0:T(8,128)}, u32[]{:S(2)}) %copy-start.1) | copy-done | bytes 1638424
  81.7 1.0 copy-done.3
  82.7 0.9 copy-done.4
  83.6 9.7 %shard_map.97 = (f32[512,128]{1,0:T(8,128)}, f32[8,128]{1,0:T(8,128)S(1)}) custom-call(f32[512,512]{1,0:T(8,128)S(1)} %copy.12.coarse, f32[512,128]{1,0:T(8,128)} %collective-permute-done.upper, f32[512,128]{1,0:T(8,128)} %collective-permute-done.1.left, f32[512,128]{1,0:T(8,128)S(1)} %copy-done.4, s32[1,384]{1,0:T(1,128)S(1)} %copy-done.8, ...), custom_call_target="tpu_custom_call" | custom-call | tf_op jit(solution)/shard_map/pallas_call | solution.py:374
  93.4 0.6 copy-done.6
  94.0 11.1 %shard_map.98 = f32[8,128]{1,0:T(8,128)} custom-call(f32[8,128]{1,0:T(8,128)} %copy-done.6), custom_call_target="tpu_custom_call" | custom-call | tf_op jit(solution)/shard_map/pallas_call | solution.py:297
  105.1 1.4 %slice_reduce_fusion = f32[6]{0:T(128)} fusion(f32[8,128]{1,0:T(8,128)} %shard_map.98), kind=kLoop, calls=%fused_computation.2 | loop fusion | bytes 48 | tf_op jit(solution)/shard_map/slice | solution.py:383
  (8 shorter events, 0.0 us)
Async XLA Ops:
  7.2 71.5 %all-gather.2.cloned.1.call-start = ((), (), s32[]{:S(2)}) async-start(), calls=%async_computation | async-start | bytes 1081344 | tf_op jit(solution)/shard_map/all_gather | solution.py:342
  7.2 73.0 %collective-permute-start = (f32[512,128]{1,0:T(8,128)}, f32[512,128]{1,0:T(8,128)}, u32[]{:S(2)}, u32[]{:S(2)}) collective-permute-start(f32[512,128]{1,0:T(8,128)} %own.1), channel_id=1, source_target_pairs={{0,8},{8,16},{16,24},{1,9},{9,17},{17,25},{2,10},{10,18},{18,26},{... | collective-permute-start | bytes 786440 | tf_op jit(solution)/shard_map/ppermute | solution.py:340
  10.3 69.9 %collective-permute-start.1 = (f32[512,128]{1,0:T(8,128)}, f32[512,128]{1,0:T(8,128)}, u32[]{:S(2)}, u32[]{:S(2)}) collective-permute-start(f32[512,128]{1,0:T(8,128)} %own.1), channel_id=1, source_target_pairs={{7,0},{0,1},{1,2},{2,3},{3,4},{4,5},{5,6},{6,7},{15,8},{8,9},{9,10... | collective-permute-start | bytes 786440 | tf_op jit(solution)/shard_map/ppermute | solution.py:341
  28.9 0.9 copy-start.5
  29.8 0.7 copy-start.7
  30.5 0.7 copy-start.9
  76.7 1.2 %copy-start = (f32[640,640]{1,0:T(8,128)}, f32[640,640]{1,0:T(8,128)S(1)}, u32[]{:S(2)}) copy-start(f32[640,640]{1,0:T(8,128)S(1)} %get-tuple-element.13.h_ref) | copy-start | bytes 4915204
  77.9 0.7 copy-start.2
  78.6 1.6 %copy-start.8 = (s32[1,384]{1,0:T(1,128)S(1)}, s32[1,384]{1,0:T(1,128)}, u32[]{:S(2)}) copy-start(s32[1,384]{1,0:T(1,128)} %cidx.3) | copy-start | bytes 4612
  78.6 1.6 %copy-start.10 = (s32[1,128]{1,0:T(1,128)S(1)}, s32[1,128]{1,0:T(1,128)}, u32[]{:S(2)}) copy-start(s32[1,128]{1,0:T(1,128)} %fidx.3) | copy-start | bytes 1540
  80.3 1.4 %copy-start.1 = (f32[640,640]{1,0:T(8,128)S(1)}, f32[640,640]{1,0:T(8,128)}, u32[]{:S(2)}) copy-start(f32[640,640]{1,0:T(8,128)} %copy-done) | copy-start | bytes 4915204
  81.7 1.0 copy-start.3
  82.7 0.9 copy-start.4
  93.4 0.6 copy-start.6
Sparse Core Ops, SparseCore 0:
  12.8 55.2 all-gather.1

commit v3 on v2

--- a/solution.py
+++ b/solution.py
@@ -25,6 +25,27 @@
     return lax.dot_general(
         a, b, (((0,), (0,)), ((), ())), precision=HIGH, preferred_element_type=F32
     )
+
+
+def halves(x):
+    high = x.astype(jnp.bfloat16)
+    return high, (x - high.astype(F32)).astype(jnp.bfloat16)
+
+
+def split_dot(a, b, dims):
+    def dot(x, y):
+        return lax.dot_general(x, y, (dims, ((), ())), preferred_element_type=F32)
+
+    (ah, al), (bh, bl) = a, b
+    return dot(ah, bh) + (dot(ah, bl) + dot(al, bh))
+
+
+def mm3(a, b):
+    return split_dot(halves(a), halves(b), ((1,), (0,)))
+
+
+def mm3_tn(a, b):
+    return split_dot(halves(a), halves(b), ((0,), (0,)))
 
 
 def rows(b):
@@ -64,8 +85,8 @@
     for b in range(count):
         part = x_ref[rows(b), :]
         if b:
-            part = part - mm_tn(u_ref[: b * BLK, b * BLK : (b + 1) * BLK], x_ref[: b * BLK, :])
-        x_ref[rows(b), :] = mm(inv_ref[rows(b), :], part)
+            part = part - mm3_tn(u_ref[: b * BLK, b * BLK : (b + 1) * BLK], x_ref[: b * BLK, :])
+        x_ref[rows(b), :] = mm3(inv_ref[rows(b), :], part)
 
 
 def model_kernel(
@@ -157,18 +178,20 @@
             part = part - mm(u_ref[rows(b), (b + 1) * BLK : lead], wt_ref[(b + 1) * BLK : lead, :])
         wt_ref[rows(b), :] = mm_tn(inv_ref[rows(b), :], part)
 
-    wt = wt_ref[...]
+    wt = halves(wt_ref[...])
 
     def slopes(r, carry):
         here = pl.ds(pl.multiple_of(r * BLK, BLK), BLK)
         for k in range(4):
             diff = xc[here, k : k + 1] - xr[k : k + 1, :]
-            h_ref[here, k * BLK : (k + 1) * BLK] = mm(c_ref[here, :] * (diff * diff), wt)
+            h_ref[here, k * BLK : (k + 1) * BLK] = split_dot(
+                halves(c_ref[here, :] * (diff * diff)), wt, ((1,), (0,))
+            )
         h_ref[here, 4 * BLK :] = nugget * wt_ref[here, :]
         return carry
 
     lax.fori_loop(0, nb, slopes, 0)
-    z_ref[...] = mm_tn(wt, h_ref[...])
+    z_ref[...] = split_dot(wt, halves(h_ref[...]), ((0,), (0,)))
     forward(u_ref, inv_ref, h_ref, lb)
 
     def h_of(i):
@@ -211,16 +234,16 @@
     hot_c = onehot(cidx[...], coarse.shape[1])
     hot_u = onehot(fidx[:, :half], upper.shape[1])
     hot_l = onehot(fidx[:, half:], left.shape[1])
-    white = mm(coarse[...], mm(hot_c, wt_ref[:nc, :]))
-    white = white + mm(upper[...], mm(hot_u, wt_ref[nc : nc + half, :]))
-    white = white + mm(left[...], mm(hot_l, wt_ref[nc + half : lead, :]))
-    white = white + mm(own[...], wt_ref[lead:, :])
+    white = mm3(coarse[...], mm3(hot_c, wt_ref[:nc, :]))
+    white = white + mm3(upper[...], mm3(hot_u, wt_ref[nc : nc + half, :]))
+    white = white + mm3(left[...], mm3(hot_l, wt_ref[nc + half : lead, :]))
+    white = white + mm3(own[...], wt_ref[lead:, :])
     white_ref[...] = white
-    m_ref[:nc, :] = mm_tn(hot_c, mm_tn(coarse[...], white))
-    m_ref[nc : nc + half, :] = mm_tn(hot_u, mm_tn(upper[...], white))
-    m_ref[nc + half :, :] = mm_tn(hot_l, mm_tn(left[...], white))
+    m_ref[:nc, :] = mm3_tn(hot_c, mm3_tn(coarse[...], white))
+    m_ref[nc : nc + half, :] = mm3_tn(hot_u, mm3_tn(upper[...], white))
+    m_ref[nc + half :, :] = mm3_tn(hot_l, mm3_tn(left[...], white))
     forward(u_ref, inv_ref, m_ref, lead // BLK)
-    gram = mm_tn(white, white)
+    gram = mm3_tn(white, white)
     eye = (
         lax.broadcasted_iota(jnp.int32, (BLK, BLK), 0)
         == lax.broadcasted_iota(jnp.int32, (BLK, BLK), 1)
@@ -366,7 +389,7 @@
             pltpu.VMEM((n, n), F32), pltpu.VMEM((BLK, 2 * BLK), F32),
             pltpu.VMEM((8, n), F32), pltpu.VMEM((n, 8), F32),
         ],
-        compiler_params=pltpu.CompilerParams(vmem_limit_bytes=40 * 1024 * 1024),
+        compiler_params=pltpu.CompilerParams(vmem_limit_bytes=16 * 1024 * 1024),
         cost_estimate=pl.CostEstimate(
             flops=60_000_000_000, bytes_accessed=8_000_000, transcendentals=2 * n * n
         ),
@@ -377,7 +400,7 @@
         in_specs=vmem(12),
         out_specs=vmem(2),
         scratch_shapes=[pltpu.VMEM((lead, BLK), F32)],
-        compiler_params=pltpu.CompilerParams(vmem_limit_bytes=40 * 1024 * 1024),
+        compiler_params=pltpu.CompilerParams(vmem_limit_bytes=16 * 1024 * 1024),
     )(all_values, upper_values, left_values, values, coarse_index, fine_index, u, inv, wt, h, z, fish)
     solved = exchanged(solve_kernel, shape(8, BLK), 1, terms)
     return (solved[:6, 6], white)

time: 114 us -> 107 us (0.939)
  Pallas kernels: 77.7 us -> 71.1 us
    pallas_call x1, Pallas kernels: 45.6 us -> 42.1 us  [body(): pl.pallas_call(functools.partial(model_kernel, float(reps), coarse_coords...]
    pallas_call x1, Pallas kernels: 9.75 us -> 6.57 us  [body(): pl.pallas_call(data_kernel, out_shape=[shape(reps, BLK), shape(8, BLK)],...]
  transfers between devices with their start and end apart: 3 -> 3, of which waited for: 0 -> 0; matrix products, arithmetic and copies ran while one was open for 4% -> 5% of each run, Pallas kernels for 50% -> 50%
where the time goes in v3:
time: 107 us
  Pallas kernels  71.1 us (66%)
  between operations  15.5 us (14%)
  local copies, waits for them, and re-layouts  12.4 us (12%)
  starting transfers between devices  5.49 us (5%)
  other arithmetic  2.19 us (2%)
    pallas_call x1, Pallas kernels, body(): pl.pallas_call(functools.partial(model_kernel, float(reps), coarse_coords...  42.1 us
    pallas_call x2, Pallas kernels, exchanged(): pl.pallas_call(kernel, out_shape=out_shape, in_specs=vmem(1), out_specs=v...  22.4 us
    unnamed x22, local copies, waits for them, and re-layouts  8.11 us
    pallas_call x1, Pallas kernels, body(): pl.pallas_call(data_kernel, out_shape=[shape(reps, BLK), shape(8, BLK)],...  6.57 us
    ppermute x1, starting transfers between devices, body(): upper_values = lax.ppermute(values, 'row', down)  3.12 us
    ppermute x1, starting transfers between devices, body(): left_values = lax.ppermute(values, 'col', across)  2.34 us
  transfers between devices with their start and end apart: 3, of which 0 were waited for; matrix products, arithmetic and copies ran while one was open for 5% of the time, Pallas kernels for 50%

profile of v3, /device:TPU:0, one launch (start us, length us, event | category | flops | bytes accessed | tf_op | source)
XLA Modules:
  0.0 106.7 jit_solution(15856409189542971741)
XLA Ops:
  7.2 0.0 all-gather.2.cloned.1.call-start
  7.2 3.1 %collective-permute-start = (f32[512,128]{1,0:T(8,128)}, f32[512,128]{1,0:T(8,128)}, u32[]{:S(2)}, u32[]{:S(2)}) collective-permute-start(f32[512,128]{1,0:T(8,128)} %own.1), channel_id=1, source_target_pairs={{0,8},{8,16},{16,24},{1,9},{9,17},{17,25},{2,10},{10,18},{18,26},{... | collective-permute-start | bytes 786440 | tf_op jit(solution)/shard_map/ppermute | solution.py:363
  10.3 2.3 %collective-permute-start.1 = (f32[512,128]{1,0:T(8,128)}, f32[512,128]{1,0:T(8,128)}, u32[]{:S(2)}, u32[]{:S(2)}) collective-permute-start(f32[512,128]{1,0:T(8,128)} %own.1), channel_id=1, source_target_pairs={{7,0},{0,1},{1,2},{2,3},{3,4},{4,5},{5,6},{6,7},{15,8},{8,9},{9,10... | collective-permute-start | bytes 786440 | tf_op jit(solution)/shard_map/ppermute | solution.py:364
  12.7 0.0 all-gather.2.cloned.1.call-update
  12.7 0.7 multiply_divide_fusion
  13.4 1.3 %fusion = (f32[1]{0:T(128)}, f32[1]{0:T(128)}) fusion(f32[6]{0:T(128)} %param.14), kind=kLoop, calls=%fused_computation.6 | loop fusion | bytes 16 | tf_op jit(solution)/shard_map/slice | solution.py:368
  16.1 1.3 %select_maximum_fusion.x_ref = f32[8,128]{1,0:T(8,128)} fusion(f32[4,16]{1,0:T(4,128)} %param.10, f32[4,128]{1,0:T(4,128)} %param.8), kind=kLoop, calls=%fused_computation | loop fusion | flops 3072 | bytes 6400 | tf_op jit(solution)/shard_map/concatenate | solution.py:359
  17.4 11.3 %shard_map.95.held = f32[32,8,128]{2,1,0:T(8,128)} custom-call(f32[8,128]{1,0:T(8,128)} %select_maximum_fusion.x_ref), custom_call_target="tpu_custom_call" | custom-call | tf_op jit(solution)/shard_map/pallas_call | solution.py:320
  28.7 0.1 pad_maximum_fusion.scal
  28.8 0.1 pad_add_fusion.where
  28.9 0.0 copy-start.5
  28.9 0.9 copy-done.5
  29.8 0.0 copy-start.7
  29.8 0.7 copy-done.7
  30.5 0.7 copy-done.9
  31.1 42.1 %shard_map.96 = (f32[640,640]{1,0:T(8,128)S(1)}, f32[640,128]{1,0:T(8,128)S(1)}, f32[640,128]{1,0:T(8,128)S(1)}, f32[640,640]{1,0:T(8,128)S(1)}, f32[128,640]{1,0:T(8,128)S(1)}, /*index=5*/f32[8,128]{1,0:T(8,128)S(1)}) custom-call(f32[6]{0:T(128)S(1)} %pad_maximum_fusion.scal, s32[4]{0:T(128)S(1)} %pad_add_fusion.where, f32[32,8,128]{2,1,0:T(8,128)S(1)} %copy-done.5, ...), custom_call_target="tpu_custom_call" | custom-call | flops 60000002048 | bytes 8000000 | tf_op jit(solution)/shard_map/pallas_call | solution.py:380
  73.3 0.0 copy-start
  73.3 1.2 %copy-done = f32[640,640]{1,0:T(8,128)} copy-done((f32[640,640]{1,0:T(8,128)}, f32[640,640]{1,0:T(8,128)S(1)}, u32[]{:S(2)}) %copy-start) | copy-done | bytes 1638424
  74.5 0.7 copy-done.2
  75.2 1.6 %copy.12.coarse = f32[512,512]{1,0:T(8,128)S(1)} copy(f32[512,512]{0,1:T(8,128)} %all-gather.2.cloned.1.call-done) | data formatting | bytes 2097152 | tf_op jit(solution)/shard_map/all_gather | solution.py:365
  76.8 0.0 collective-permute-done.upper
  76.8 0.0 collective-permute-done.1.left
  76.8 0.0 copy-done.8
  76.8 0.0 copy-done.10
  76.8 0.0 copy-start.1
  76.8 1.4 %copy-done.1 = f32[640,640]{1,0:T(8,128)S(1)} copy-done((f32[640,640]{1,0:T(8,128)S(1)}, f32[640,640]{1,0:T(8,128)}, u32[]{:S(2)}) %copy-start.1) | copy-done | bytes 1638424
  78.3 1.0 copy-done.3
  79.2 0.9 copy-done.4
  80.2 6.6 %shard_map.97 = (f32[512,128]{1,0:T(8,128)}, f32[8,128]{1,0:T(8,128)S(1)}) custom-call(f32[512,512]{1,0:T(8,128)S(1)} %copy.12.coarse, f32[512,128]{1,0:T(8,128)} %collective-permute-done.upper, f32[512,128]{1,0:T(8,128)} %collective-permute-done.1.left, f32[512,128]{1,0:T(8,128)S(1)} %copy-done.4, s32[1,384]{1,0:T(1,128)S(1)} %copy-done.8, ...), custom_call_target="tpu_custom_call" | custom-call | tf_op jit(solution)/shard_map/pallas_call | solution.py:397
  86.8 0.6 copy-done.6
  87.3 11.1 %shard_map.98 = f32[8,128]{1,0:T(8,128)} custom-call(f32[8,128]{1,0:T(8,128)} %copy-done.6), custom_call_target="tpu_custom_call" | custom-call | tf_op jit(solution)/shard_map/pallas_call | solution.py:320
  98.5 1.4 %slice_reduce_fusion = f32[6]{0:T(128)} fusion(f32[8,128]{1,0:T(8,128)} %shard_map.98), kind=kLoop, calls=%fused_computation.2 | loop fusion | bytes 48 | tf_op jit(solution)/shard_map/slice | solution.py:406
  (8 shorter events, 0.0 us)
Async XLA Ops:
  7.2 68.0 %all-gather.2.cloned.1.call-start = ((), (), s32[]{:S(2)}) async-start(), calls=%async_computation | async-start | bytes 1081344 | tf_op jit(solution)/shard_map/all_gather | solution.py:365
  7.2 69.6 %collective-permute-start = (f32[512,128]{1,0:T(8,128)}, f32[512,128]{1,0:T(8,128)}, u32[]{:S(2)}, u32[]{:S(2)}) collective-permute-start(f32[512,128]{1,0:T(8,128)} %own.1), channel_id=1, source_target_pairs={{0,8},{8,16},{16,24},{1,9},{9,17},{17,25},{2,10},{10,18},{18,26},{... | collective-permute-start | bytes 786440 | tf_op jit(solution)/shard_map/ppermute | solution.py:363
  10.3 66.5 %collective-permute-start.1 = (f32[512,128]{1,0:T(8,128)}, f32[512,128]{1,0:T(8,128)}, u32[]{:S(2)}, u32[]{:S(2)}) collective-permute-start(f32[512,128]{1,0:T(8,128)} %own.1), channel_id=1, source_target_pairs={{7,0},{0,1},{1,2},{2,3},{3,4},{4,5},{5,6},{6,7},{15,8},{8,9},{9,10... | collective-permute-start | bytes 786440 | tf_op jit(solution)/shard_map/ppermute | solution.py:364
  28.9 0.9 copy-start.5
  29.8 0.7 copy-start.7
  30.5 0.7 copy-start.9
  73.3 1.2 %copy-start = (f32[640,640]{1,0:T(8,128)}, f32[640,640]{1,0:T(8,128)S(1)}, u32[]{:S(2)}) copy-start(f32[640,640]{1,0:T(8,128)S(1)} %get-tuple-element.13.h_ref) | copy-start | bytes 4915204
  74.5 0.7 copy-start.2
  75.2 1.6 %copy-start.8 = (s32[1,384]{1,0:T(1,128)S(1)}, s32[1,384]{1,0:T(1,128)}, u32[]{:S(2)}) copy-start(s32[1,384]{1,0:T(1,128)} %cidx.3) | copy-start | bytes 4612
  75.2 1.6 %copy-start.10 = (s32[1,128]{1,0:T(1,128)S(1)}, s32[1,128]{1,0:T(1,128)}, u32[]{:S(2)}) copy-start(s32[1,128]{1,0:T(1,128)} %fidx.3) | copy-start | bytes 1540
  76.8 1.4 %copy-start.1 = (f32[640,640]{1,0:T(8,128)S(1)}, f32[640,640]{1,0:T(8,128)}, u32[]{:S(2)}) copy-start(f32[640,640]{1,0:T(8,128)} %copy-done) | copy-start | bytes 4915204
  78.3 1.0 copy-start.3
  79.2 0.9 copy-start.4
  86.7 0.6 copy-start.6
Sparse Core Ops, SparseCore 0:
  12.8 55.2 all-gather.1
